TPU v7x, 256 devices: a whole 4x4x8 slice. The times are simulated.
256 devices in a mesh: tgt: 32 (over z, y_hi, core), src: 8 (over y_lo, x).
Axes of the slice: x: 4, y: 4 (y_hi: 2, y_lo: 2; y = y_hi * 2 + y_lo), z: 8, core: 2. Of those that a mesh axis runs over, the one named last changes fastest.
Arguments:
- tgt_points: bfloat16 [3, 16384], P(None, 'tgt'), may hold values from -4 to 4
- tgt_weight: float32 [16384], P('tgt'), may hold values from 0.5 to 2
- src_points: bfloat16 [4, 3, 32768], P(None, None, ('tgt', 'src')), may hold values from -4 to 4
- src_weight: float32 [4, 32768], P(None, ('tgt', 'src')), may hold values from 0.5 to 2
- basis: float32 [4, 3, 32768], P(None, None, ('tgt', 'src')), may hold values from 0.05 to 1
- span: int32 [4, 32768], P(None, ('tgt', 'src')), may hold values from 0 to 29
- patch: int32 [4, 32768], P(None, ('tgt', 'src')), may hold values from 0 to 3
- patch_factor: float32 [4, 2, 1024], P(None, None, ('tgt', 'src')), may hold values from -1.5 to 1.5
- ctrl_weight: float32 [4, 8192], P(None, ('tgt', 'src')), may hold values from 0.5 to 2
- ctrl_coef: bfloat16 [4, 128, 8192], P(None, None, ('tgt', 'src')), may hold values from -6 to 6
- band: float32 [8, 16384], P(None, 'tgt'), may hold values from -0.5 to 0.5
- offsets: int32 [8], replicated, may hold values from -8 to 8, as said below
Outputs:
- shell_field: float32 [16384, 128], P('tgt')
Inputs may be any that keep to these rules, and one draw needn't show every extreme that they name: span of source point j is local to the 32 control points of the block j // 128. patch of source point j is local to the 4 patches of the block j // 128. offsets[0] is 8 and offsets[1] is -8.
All inputs are finite; a program needn't handle non-finite values.
Results may differ from a plain program's by a relative error of at most 0.0041.
Values may be sent and summed in bfloat16 or wider, within the bound.
No kernel may reach another device: no remote copies, remote signals or barrier semaphores. Data moves between devices by JAX's collectives and lax.ppermute only.
A program may use at most 128 MiB of HBM per device.

v0:
```python
import math
import jax
import jax.numpy as jnp
from jax import lax
from jax.sharding import PartitionSpec as P

HALO = 8
WAVE = 8.0
SMOOTH = 0.0025


def extended(block, sides, width):
    for axis, dim in sides:
        count = lax.axis_size(axis)
        forward = [(i, i + 1) for i in range(count - 1)]
        backward = [(target, source) for source, target in forward]
        low = lax.ppermute(
            lax.slice_in_dim(block, block.shape[dim] - width, None, axis=dim), axis, forward
        )
        high = lax.ppermute(lax.slice_in_dim(block, 0, width, axis=dim), axis, backward)
        block = jnp.concatenate([low, block, high], axis=dim)
    return block


def kernel_terms(targets, sources, density):
    tpos = targets.astype(jnp.float32)
    spos = sources.astype(jnp.float32)
    dist_sq = SMOOTH + (tpos[0][:, None] - spos[0][None, :]) ** 2
    dist_sq = dist_sq + (tpos[1][:, None] - spos[1][None, :]) ** 2
    dist_sq = dist_sq + (tpos[2][:, None] - spos[2][None, :]) ** 2
    dist = jnp.sqrt(dist_sq)
    kernel_re = (jnp.cos(WAVE * dist) / dist).astype(jnp.bfloat16)
    kernel_im = (jnp.sin(WAVE * dist) / dist).astype(jnp.bfloat16)
    dims = (((1,), (1,)), ((), ()))
    part_a = lax.dot_general(kernel_re, density, dims, preferred_element_type=jnp.float32)
    part_b = lax.dot_general(kernel_im, density, dims, preferred_element_type=jnp.float32)
    half = density.shape[0] // 2
    return jnp.concatenate(
        [part_a[:, :half] - part_b[:, half:], part_a[:, half:] + part_b[:, :half]], axis=1
    )


def block_density(weight, basis_rows, span_row, patch_row, factor_rows, weights_ctrl, coef_ctrl):
    count = weight.shape[0]
    fields = coef_ctrl.shape[0] // 2
    denom = jnp.zeros((count,), jnp.float32)
    numer = jnp.zeros((coef_ctrl.shape[0], count), jnp.float32)
    for basis_index in range(basis_rows.shape[0]):
        control_index = span_row + basis_index
        scaled = basis_rows[basis_index] * weights_ctrl[control_index]
        denom = denom + scaled
        numer = numer + scaled[None, :] * coef_ctrl[:, control_index].astype(jnp.float32)
    ratio = numer / denom[None, :]
    labels = jnp.arange(factor_rows.shape[1], dtype=jnp.int32)
    member = patch_row[None, :] == labels[:, None]
    factor_re = jnp.sum(jnp.where(member, factor_rows[0][:, None], 0.0), axis=0)
    factor_im = jnp.sum(jnp.where(member, factor_rows[1][:, None], 0.0), axis=0)
    ratio_re = ratio[:fields]
    ratio_im = ratio[fields:]
    dens_re = weight * (factor_re * ratio_re - factor_im * ratio_im)
    dens_im = weight * (factor_re * ratio_im + factor_im * ratio_re)
    return jnp.concatenate([dens_re, dens_im], axis=0).astype(jnp.bfloat16)


def add_kernel(carried, targets, geometry, density):
    width = geometry.shape[1]
    block_size = 1024

    def step_fn(index, inner):
        begin = index * block_size
        part_geo = lax.dynamic_slice_in_dim(geometry, begin, block_size, 1)
        part_den = lax.dynamic_slice_in_dim(density, begin, block_size, 1)
        return inner + kernel_terms(targets, part_geo, part_den)

    return lax.fori_loop(0, width // block_size, step_fn, carried)


def per_device(
    tgt_points,
    tgt_weight,
    src_points,
    src_weight,
    basis,
    span,
    patch,
    patch_factor,
    ctrl_weight,
    ctrl_coef,
    band,
    offsets,
):
    rows = tgt_points.shape[1]
    columns = ctrl_coef.shape[1]
    rounds = src_weight.shape[0]
    partial_value = jnp.zeros((rows, columns), jnp.float32)
    for section in range(rounds):
        density = block_density(
            src_weight[section],
            basis[section],
            span[section],
            patch[section],
            patch_factor[section],
            ctrl_weight[section],
            ctrl_coef[section],
        )
        geometry, gathered = (
            lax.all_gather(src_points[section], "tgt", axis=1, tiled=True),
            lax.all_gather(density, "tgt", axis=1, tiled=True),
        )
        partial_value = add_kernel(partial_value, tgt_points, geometry, gathered)
    total = lax.psum(partial_value, "src")
    source_count = rounds * src_weight.shape[1] * lax.axis_size("tgt") * lax.axis_size("src")
    scale = jnp.float32(1.0 / math.sqrt(source_count))
    potential = total * scale * tgt_weight[:, None]
    padded = extended(potential, (("tgt", 0),), HALO)
    shell_field = potential
    for diag in range(band.shape[0]):
        begin = HALO + offsets[diag]
        shifted = lax.dynamic_slice_in_dim(padded, begin, rows, 0)
        shell_field = shell_field + band[diag][:, None] * shifted
    return shell_field


def solution(mesh):
    in_specs = (
        P(None, "tgt"),
        P("tgt"),
        P(None, None, ("tgt", "src")),
        P(None, ("tgt", "src")),
        P(None, None, ("tgt", "src")),
        P(None, ("tgt", "src")),
        P(None, ("tgt", "src")),
        P(None, None, ("tgt", "src")),
        P(None, ("tgt", "src")),
        P(None, None, ("tgt", "src")),
        P(None, "tgt"),
        P(),
    )
    out_specs = P("tgt", None)
    return jax.shard_map(
        per_device, mesh=mesh, in_specs=in_specs, out_specs=out_specs, check_vma=False
    )
```

profile of v0, /device:TPU:1, one launch (start us, length us, event | category | flops | bytes accessed | tf_op | source)
XLA Modules:
  0.0 627.5 jit_solution(9285904822959095373)
XLA Ops:
  6.5 0.7 slice_bitcast_fusion
  7.3 0.8 fusion.49
  9.6 0.8 slice_bitcast_fusion.5
  10.4 1.2 gather_fusion.4
  11.6 1.2 gather_fusion.2
  13.6 1.2 gather_fusion
  15.2 1.2 gather_fusion.20
  16.4 1.2 gather_fusion.18
  17.7 1.2 gather_fusion.22
  19.0 1.2 gather_fusion.10
  20.2 1.2 gather_fusion.8
  21.4 1.2 gather_fusion.6
  23.6 0.7 gather_fusion.11
  26.9 0.7 gather_fusion.15
  28.3 1.2 gather_fusion.14
  29.6 1.2 gather_fusion.12
  31.5 1.2 gather_fusion.16
  34.0 0.7 gather_fusion.23
  37.3 46.2 %all-gather = bf16[1,3,4096]{2,1,0:T(4,128)(2,1)S(1)} all-gather(bf16[1,3,128]{2,1,0:T(4,128)(2,1)S(1)} %copy.57), channel_id=2, replica_groups=mesh['tgt'=32,'src'=8] {'tgt'}, dimensions={2}, use_global_device_ids=true | all-gather | bytes 25344 | tf_op jit(solution)/shard_map/all_gather | solution.py:107
  83.5 36.7 %all-gather.1 = bf16[1,3,4096]{2,1,0:T(4,128)(2,1)S(1)} all-gather(bf16[1,3,128]{2,1,0:T(4,128)(2,1)S(1)} %copy.58), channel_id=3, replica_groups=mesh['tgt'=32,'src'=8] {'tgt'}, dimensions={2}, use_global_device_ids=true | all-gather | bytes 25344 | tf_op jit(solution)/shard_map/all_gather | solution.py:107
  120.2 39.6 %all-gather.2 = bf16[1,3,4096]{2,1,0:T(4,128)(2,1)S(1)} all-gather(bf16[1,3,128]{2,1,0:T(4,128)(2,1)S(1)} %copy.59), channel_id=4, replica_groups=mesh['tgt'=32,'src'=8] {'tgt'}, dimensions={2}, use_global_device_ids=true | all-gather | bytes 25344 | tf_op jit(solution)/shard_map/all_gather | solution.py:107
  159.8 36.7 %all-gather.3 = bf16[1,3,4096]{2,1,0:T(4,128)(2,1)S(1)} all-gather(bf16[1,3,128]{2,1,0:T(4,128)(2,1)S(1)} %copy.60), channel_id=5, replica_groups=mesh['tgt'=32,'src'=8] {'tgt'}, dimensions={2}, use_global_device_ids=true | all-gather | bytes 25344 | tf_op jit(solution)/shard_map/all_gather | solution.py:107
  196.5 78.8 %while.56 = (s32[]{:T(128)}, f32[512,128]{0,1:T(8,128)S(1)}, bf16[3,512]{1,0:T(4,128)(2,1)S(1)}, bf16[3,4096]{1,0:T(4,128)(2,1)S(1)}, bf16[128,4096]{1,0:T(8,128...) while((s32[]{:T(128)}, f32[512,128]{0,1:T(8,128)S(1)}, bf16[3,512]{1,0:T(4,128)(2,1)S(1)}, ...), condition=%wide.region_3.4_spmd.clone, body=%wide.region_2.3_spmd.clone.sunk | while | flops 281283584 | bytes 2713769 | solution.py:75
  196.7 9.7 %fusion.110 = f32[512,128]{0,1:T(8,128)S(1)} fusion(f32[1024]{0:T(1024)S(1)} %bitcast.278, f32[512]{0:T(512)S(1)} %bitcast.304, f32[1024]{0:T(1024)S(1)} %bitcast.280, f32[512]{0:T(512)S(1)} %bitcast.302, f32[1024]{0:T(1024)S(1)} %bitcast.276, f32[512]{0:T(512)S(1)} %bitcast.300, bf16[128,4096]{1,0:T(8,128)(2,1)} %get-tuple-element.859, ...), kind=kOutput, calls=%fused_computation.79.clone.1 | convolution fusion | flops 140509184 | bytes 542724 | tf_op jit(solution)/shard_map/while/body/eval_jaxpr/dot_general | solution.py:36
  206.4 9.6 %fusion.111 = f32[512,128]{0,1:T(8,128)S(1)} fusion(f32[1024]{0:T(1024)S(1)} %bitcast.279, f32[512]{0:T(512)S(1)} %bitcast.305, f32[1024]{0:T(1024)S(1)} %bitcast.281, f32[512]{0:T(512)S(1)} %bitcast.303, f32[1024]{0:T(1024)S(1)} %bitcast.277, f32[512]{0:T(512)S(1)} %bitcast.301, bf16[128,4096]{1,0:T(8,128)(2,1)} %get-tuple-element.859, ...), kind=kOutput, calls=%fused_computation.78.clone.1 | convolution fusion | flops 140509184 | bytes 542724 | tf_op jit(solution)/shard_map/while/body/eval_jaxpr/dot_general | solution.py:35
  216.3 9.7 %fusion.110 = f32[512,128]{0,1:T(8,128)S(1)} fusion(f32[1024]{0:T(1024)S(1)} %bitcast.278, f32[512]{0:T(512)S(1)} %bitcast.304, f32[1024]{0:T(1024)S(1)} %bitcast.280, f32[512]{0:T(512)S(1)} %bitcast.302, f32[1024]{0:T(1024)S(1)} %bitcast.276, f32[512]{0:T(512)S(1)} %bitcast.300, bf16[128,4096]{1,0:T(8,128)(2,1)} %get-tuple-element.859, ...), kind=kOutput, calls=%fused_computation.79.clone.1 | convolution fusion | flops 140509184 | bytes 542724 | tf_op jit(solution)/shard_map/while/body/eval_jaxpr/dot_general | solution.py:36
  226.0 9.6 %fusion.111 = f32[512,128]{0,1:T(8,128)S(1)} fusion(f32[1024]{0:T(1024)S(1)} %bitcast.279, f32[512]{0:T(512)S(1)} %bitcast.305, f32[1024]{0:T(1024)S(1)} %bitcast.281, f32[512]{0:T(512)S(1)} %bitcast.303, f32[1024]{0:T(1024)S(1)} %bitcast.277, f32[512]{0:T(512)S(1)} %bitcast.301, bf16[128,4096]{1,0:T(8,128)(2,1)} %get-tuple-element.859, ...), kind=kOutput, calls=%fused_computation.78.clone.1 | convolution fusion | flops 140509184 | bytes 542724 | tf_op jit(solution)/shard_map/while/body/eval_jaxpr/dot_general | solution.py:35
  235.8 9.7 %fusion.110 = f32[512,128]{0,1:T(8,128)S(1)} fusion(f32[1024]{0:T(1024)S(1)} %bitcast.278, f32[512]{0:T(512)S(1)} %bitcast.304, f32[1024]{0:T(1024)S(1)} %bitcast.280, f32[512]{0:T(512)S(1)} %bitcast.302, f32[1024]{0:T(1024)S(1)} %bitcast.276, f32[512]{0:T(512)S(1)} %bitcast.300, bf16[128,4096]{1,0:T(8,128)(2,1)} %get-tuple-element.859, ...), kind=kOutput, calls=%fused_computation.79.clone.1 | convolution fusion | flops 140509184 | bytes 542724 | tf_op jit(solution)/shard_map/while/body/eval_jaxpr/dot_general | solution.py:36
  245.5 9.6 %fusion.111 = f32[512,128]{0,1:T(8,128)S(1)} fusion(f32[1024]{0:T(1024)S(1)} %bitcast.279, f32[512]{0:T(512)S(1)} %bitcast.305, f32[1024]{0:T(1024)S(1)} %bitcast.281, f32[512]{0:T(512)S(1)} %bitcast.303, f32[1024]{0:T(1024)S(1)} %bitcast.277, f32[512]{0:T(512)S(1)} %bitcast.301, bf16[128,4096]{1,0:T(8,128)(2,1)} %get-tuple-element.859, ...), kind=kOutput, calls=%fused_computation.78.clone.1 | convolution fusion | flops 140509184 | bytes 542724 | tf_op jit(solution)/shard_map/while/body/eval_jaxpr/dot_general | solution.py:35
  255.4 9.7 %fusion.110 = f32[512,128]{0,1:T(8,128)S(1)} fusion(f32[1024]{0:T(1024)S(1)} %bitcast.278, f32[512]{0:T(512)S(1)} %bitcast.304, f32[1024]{0:T(1024)S(1)} %bitcast.280, f32[512]{0:T(512)S(1)} %bitcast.302, f32[1024]{0:T(1024)S(1)} %bitcast.276, f32[512]{0:T(512)S(1)} %bitcast.300, bf16[128,4096]{1,0:T(8,128)(2,1)} %get-tuple-element.859, ...), kind=kOutput, calls=%fused_computation.79.clone.1 | convolution fusion | flops 140509184 | bytes 542724 | tf_op jit(solution)/shard_map/while/body/eval_jaxpr/dot_general | solution.py:36
  265.1 9.6 %fusion.111 = f32[512,128]{0,1:T(8,128)S(1)} fusion(f32[1024]{0:T(1024)S(1)} %bitcast.279, f32[512]{0:T(512)S(1)} %bitcast.305, f32[1024]{0:T(1024)S(1)} %bitcast.281, f32[512]{0:T(512)S(1)} %bitcast.303, f32[1024]{0:T(1024)S(1)} %bitcast.277, f32[512]{0:T(512)S(1)} %bitcast.301, bf16[128,4096]{1,0:T(8,128)(2,1)} %get-tuple-element.859, ...), kind=kOutput, calls=%fused_computation.78.clone.1 | convolution fusion | flops 140509184 | bytes 542724 | tf_op jit(solution)/shard_map/while/body/eval_jaxpr/dot_general | solution.py:35
  275.3 78.1 %while.53 = (s32[]{:T(128)}, f32[512,128]{0,1:T(8,128)S(1)}, bf16[3,512]{1,0:T(4,128)(2,1)S(1)}, bf16[3,4096]{1,0:T(4,128)(2,1)S(1)}, bf16[128,4096]{1,0:T(8,128...) while((s32[]{:T(128)}, f32[512,128]{0,1:T(8,128)S(1)}, bf16[3,512]{1,0:T(4,128)(2,1)S(1)}, ...), condition=%wide.region_7.8_spmd, body=%wide.region_6.7_spmd.sunk | while | flops 281218048 | bytes 2713759 | solution.py:75
  275.4 9.7 %fusion.92 = f32[512,128]{0,1:T(8,128)S(1)} fusion(f32[1024]{0:T(1024)S(1)} %bitcast.284, f32[512]{0:T(512)S(1)} %bitcast.310, f32[1024]{0:T(1024)S(1)} %bitcast.286, f32[512]{0:T(512)S(1)} %bitcast.308, f32[1024]{0:T(1024)S(1)} %bitcast.282, f32[512]{0:T(512)S(1)} %bitcast.306, bf16[128,4096]{1,0:T(8,128)(2,1)} %get-tuple-element.886, ...), kind=kOutput, calls=%fused_computation.28.clone.1 | convolution fusion | flops 140509184 | bytes 542724 | tf_op jit(solution)/shard_map/while/body/eval_jaxpr/dot_general | solution.py:36
  285.1 9.6 %fusion.93 = f32[512,128]{0,1:T(8,128)S(1)} fusion(f32[1024]{0:T(1024)S(1)} %bitcast.285, f32[512]{0:T(512)S(1)} %bitcast.311, f32[1024]{0:T(1024)S(1)} %bitcast.287, f32[512]{0:T(512)S(1)} %bitcast.309, f32[1024]{0:T(1024)S(1)} %bitcast.283, f32[512]{0:T(512)S(1)} %bitcast.307, bf16[128,4096]{1,0:T(8,128)(2,1)} %get-tuple-element.886, ...), kind=kOutput, calls=%fused_computation.27.clone.1 | convolution fusion | flops 140509184 | bytes 542724 | tf_op jit(solution)/shard_map/while/body/eval_jaxpr/dot_general | solution.py:35
  294.9 9.7 %fusion.92 = f32[512,128]{0,1:T(8,128)S(1)} fusion(f32[1024]{0:T(1024)S(1)} %bitcast.284, f32[512]{0:T(512)S(1)} %bitcast.310, f32[1024]{0:T(1024)S(1)} %bitcast.286, f32[512]{0:T(512)S(1)} %bitcast.308, f32[1024]{0:T(1024)S(1)} %bitcast.282, f32[512]{0:T(512)S(1)} %bitcast.306, bf16[128,4096]{1,0:T(8,128)(2,1)} %get-tuple-element.886, ...), kind=kOutput, calls=%fused_computation.28.clone.1 | convolution fusion | flops 140509184 | bytes 542724 | tf_op jit(solution)/shard_map/while/body/eval_jaxpr/dot_general | solution.py:36
  304.6 9.6 %fusion.93 = f32[512,128]{0,1:T(8,128)S(1)} fusion(f32[1024]{0:T(1024)S(1)} %bitcast.285, f32[512]{0:T(512)S(1)} %bitcast.311, f32[1024]{0:T(1024)S(1)} %bitcast.287, f32[512]{0:T(512)S(1)} %bitcast.309, f32[1024]{0:T(1024)S(1)} %bitcast.283, f32[512]{0:T(512)S(1)} %bitcast.307, bf16[128,4096]{1,0:T(8,128)(2,1)} %get-tuple-element.886, ...), kind=kOutput, calls=%fused_computation.27.clone.1 | convolution fusion | flops 140509184 | bytes 542724 | tf_op jit(solution)/shard_map/while/body/eval_jaxpr/dot_general | solution.py:35
  314.5 9.7 %fusion.92 = f32[512,128]{0,1:T(8,128)S(1)} fusion(f32[1024]{0:T(1024)S(1)} %bitcast.284, f32[512]{0:T(512)S(1)} %bitcast.310, f32[1024]{0:T(1024)S(1)} %bitcast.286, f32[512]{0:T(512)S(1)} %bitcast.308, f32[1024]{0:T(1024)S(1)} %bitcast.282, f32[512]{0:T(512)S(1)} %bitcast.306, bf16[128,4096]{1,0:T(8,128)(2,1)} %get-tuple-element.886, ...), kind=kOutput, calls=%fused_computation.28.clone.1 | convolution fusion | flops 140509184 | bytes 542724 | tf_op jit(solution)/shard_map/while/body/eval_jaxpr/dot_general | solution.py:36
  324.1 9.6 %fusion.93 = f32[512,128]{0,1:T(8,128)S(1)} fusion(f32[1024]{0:T(1024)S(1)} %bitcast.285, f32[512]{0:T(512)S(1)} %bitcast.311, f32[1024]{0:T(1024)S(1)} %bitcast.287, f32[512]{0:T(512)S(1)} %bitcast.309, f32[1024]{0:T(1024)S(1)} %bitcast.283, f32[512]{0:T(512)S(1)} %bitcast.307, bf16[128,4096]{1,0:T(8,128)(2,1)} %get-tuple-element.886, ...), kind=kOutput, calls=%fused_computation.27.clone.1 | convolution fusion | flops 140509184 | bytes 542724 | tf_op jit(solution)/shard_map/while/body/eval_jaxpr/dot_general | solution.py:35
  334.0 9.7 %fusion.92 = f32[512,128]{0,1:T(8,128)S(1)} fusion(f32[1024]{0:T(1024)S(1)} %bitcast.284, f32[512]{0:T(512)S(1)} %bitcast.310, f32[1024]{0:T(1024)S(1)} %bitcast.286, f32[512]{0:T(512)S(1)} %bitcast.308, f32[1024]{0:T(1024)S(1)} %bitcast.282, f32[512]{0:T(512)S(1)} %bitcast.306, bf16[128,4096]{1,0:T(8,128)(2,1)} %get-tuple-element.886, ...), kind=kOutput, calls=%fused_computation.28.clone.1 | convolution fusion | flops 140509184 | bytes 542724 | tf_op jit(solution)/shard_map/while/body/eval_jaxpr/dot_general | solution.py:36
  343.7 9.6 %fusion.93 = f32[512,128]{0,1:T(8,128)S(1)} fusion(f32[1024]{0:T(1024)S(1)} %bitcast.285, f32[512]{0:T(512)S(1)} %bitcast.311, f32[1024]{0:T(1024)S(1)} %bitcast.287, f32[512]{0:T(512)S(1)} %bitcast.309, f32[1024]{0:T(1024)S(1)} %bitcast.283, f32[512]{0:T(512)S(1)} %bitcast.307, bf16[128,4096]{1,0:T(8,128)(2,1)} %get-tuple-element.886, ...), kind=kOutput, calls=%fused_computation.27.clone.1 | convolution fusion | flops 140509184 | bytes 542724 | tf_op jit(solution)/shard_map/while/body/eval_jaxpr/dot_general | solution.py:35
  353.5 78.3 %while.54 = (s32[]{:T(128)}, f32[512,128]{0,1:T(8,128)S(1)}, bf16[3,512]{1,0:T(4,128)(2,1)S(1)}, bf16[3,4096]{1,0:T(4,128)(2,1)S(1)}, bf16[128,4096]{1,0:T(8,128...) while((s32[]{:T(128)}, f32[512,128]{0,1:T(8,128)S(1)}, bf16[3,512]{1,0:T(4,128)(2,1)S(1)}, ...), condition=%wide.region_11.12_spmd, body=%wide.region_10.11_spmd.sunk | while | flops 281218048 | bytes 2713759 | solution.py:75
  353.7 9.7 %fusion.98 = f32[512,128]{0,1:T(8,128)S(1)} fusion(f32[1024]{0:T(1024)S(1)} %bitcast.290, f32[512]{0:T(512)S(1)} %bitcast.316, f32[1024]{0:T(1024)S(1)} %bitcast.292, f32[512]{0:T(512)S(1)} %bitcast.314, f32[1024]{0:T(1024)S(1)} %bitcast.288, f32[512]{0:T(512)S(1)} %bitcast.312, bf16[128,4096]{1,0:T(8,128)(2,1)} %get-tuple-element.913, ...), kind=kOutput, calls=%fused_computation.45.clone.1 | convolution fusion | flops 140509184 | bytes 542724 | tf_op jit(solution)/shard_map/while/body/eval_jaxpr/dot_general | solution.py:36
  363.4 9.6 %fusion.99 = f32[512,128]{0,1:T(8,128)S(1)} fusion(f32[1024]{0:T(1024)S(1)} %bitcast.291, f32[512]{0:T(512)S(1)} %bitcast.317, f32[1024]{0:T(1024)S(1)} %bitcast.293, f32[512]{0:T(512)S(1)} %bitcast.315, f32[1024]{0:T(1024)S(1)} %bitcast.289, f32[512]{0:T(512)S(1)} %bitcast.313, bf16[128,4096]{1,0:T(8,128)(2,1)} %get-tuple-element.913, ...), kind=kOutput, calls=%fused_computation.44.clone.1 | convolution fusion | flops 140509184 | bytes 542724 | tf_op jit(solution)/shard_map/while/body/eval_jaxpr/dot_general | solution.py:35
  373.3 9.7 %fusion.98 = f32[512,128]{0,1:T(8,128)S(1)} fusion(f32[1024]{0:T(1024)S(1)} %bitcast.290, f32[512]{0:T(512)S(1)} %bitcast.316, f32[1024]{0:T(1024)S(1)} %bitcast.292, f32[512]{0:T(512)S(1)} %bitcast.314, f32[1024]{0:T(1024)S(1)} %bitcast.288, f32[512]{0:T(512)S(1)} %bitcast.312, bf16[128,4096]{1,0:T(8,128)(2,1)} %get-tuple-element.913, ...), kind=kOutput, calls=%fused_computation.45.clone.1 | convolution fusion | flops 140509184 | bytes 542724 | tf_op jit(solution)/shard_map/while/body/eval_jaxpr/dot_general | solution.py:36
  383.0 9.6 %fusion.99 = f32[512,128]{0,1:T(8,128)S(1)} fusion(f32[1024]{0:T(1024)S(1)} %bitcast.291, f32[512]{0:T(512)S(1)} %bitcast.317, f32[1024]{0:T(1024)S(1)} %bitcast.293, f32[512]{0:T(512)S(1)} %bitcast.315, f32[1024]{0:T(1024)S(1)} %bitcast.289, f32[512]{0:T(512)S(1)} %bitcast.313, bf16[128,4096]{1,0:T(8,128)(2,1)} %get-tuple-element.913, ...), kind=kOutput, calls=%fused_computation.44.clone.1 | convolution fusion | flops 140509184 | bytes 542724 | tf_op jit(solution)/shard_map/while/body/eval_jaxpr/dot_general | solution.py:35
  392.8 9.7 %fusion.98 = f32[512,128]{0,1:T(8,128)S(1)} fusion(f32[1024]{0:T(1024)S(1)} %bitcast.290, f32[512]{0:T(512)S(1)} %bitcast.316, f32[1024]{0:T(1024)S(1)} %bitcast.292, f32[512]{0:T(512)S(1)} %bitcast.314, f32[1024]{0:T(1024)S(1)} %bitcast.288, f32[512]{0:T(512)S(1)} %bitcast.312, bf16[128,4096]{1,0:T(8,128)(2,1)} %get-tuple-element.913, ...), kind=kOutput, calls=%fused_computation.45.clone.1 | convolution fusion | flops 140509184 | bytes 542724 | tf_op jit(solution)/shard_map/while/body/eval_jaxpr/dot_general | solution.py:36
  402.5 9.6 %fusion.99 = f32[512,128]{0,1:T(8,128)S(1)} fusion(f32[1024]{0:T(1024)S(1)} %bitcast.291, f32[512]{0:T(512)S(1)} %bitcast.317, f32[1024]{0:T(1024)S(1)} %bitcast.293, f32[512]{0:T(512)S(1)} %bitcast.315, f32[1024]{0:T(1024)S(1)} %bitcast.289, f32[512]{0:T(512)S(1)} %bitcast.313, bf16[128,4096]{1,0:T(8,128)(2,1)} %get-tuple-element.913, ...), kind=kOutput, calls=%fused_computation.44.clone.1 | convolution fusion | flops 140509184 | bytes 542724 | tf_op jit(solution)/shard_map/while/body/eval_jaxpr/dot_general | solution.py:35
  412.3 9.7 %fusion.98 = f32[512,128]{0,1:T(8,128)S(1)} fusion(f32[1024]{0:T(1024)S(1)} %bitcast.290, f32[512]{0:T(512)S(1)} %bitcast.316, f32[1024]{0:T(1024)S(1)} %bitcast.292, f32[512]{0:T(512)S(1)} %bitcast.314, f32[1024]{0:T(1024)S(1)} %bitcast.288, f32[512]{0:T(512)S(1)} %bitcast.312, bf16[128,4096]{1,0:T(8,128)(2,1)} %get-tuple-element.913, ...), kind=kOutput, calls=%fused_computation.45.clone.1 | convolution fusion | flops 140509184 | bytes 542724 | tf_op jit(solution)/shard_map/while/body/eval_jaxpr/dot_general | solution.py:36
  422.0 9.6 %fusion.99 = f32[512,128]{0,1:T(8,128)S(1)} fusion(f32[1024]{0:T(1024)S(1)} %bitcast.291, f32[512]{0:T(512)S(1)} %bitcast.317, f32[1024]{0:T(1024)S(1)} %bitcast.293, f32[512]{0:T(512)S(1)} %bitcast.315, f32[1024]{0:T(1024)S(1)} %bitcast.289, f32[512]{0:T(512)S(1)} %bitcast.313, bf16[128,4096]{1,0:T(8,128)(2,1)} %get-tuple-element.913, ...), kind=kOutput, calls=%fused_computation.44.clone.1 | convolution fusion | flops 140509184 | bytes 542724 | tf_op jit(solution)/shard_map/while/body/eval_jaxpr/dot_general | solution.py:35
  431.8 91.2 %while.55 = (s32[]{:T(128)}, f32[512,128]{0,1:T(8,128)S(1)}, bf16[3,512]{1,0:T(4,128)(2,1)S(1)}, bf16[3,4096]{1,0:T(4,128)(2,1)S(1)}, bf16[128,4096]{1,0:T(8,128...) while((s32[]{:T(128)}, f32[512,128]{0,1:T(8,128)S(1)}, bf16[3,512]{1,0:T(4,128)(2,1)S(1)}, ...), condition=%wide.region_15.16_spmd, body=%wide.region_14.15_spmd.sunk | while | flops 281218048 | bytes 2713759 | solution.py:75
  445.0 9.7 %fusion.104 = f32[512,128]{0,1:T(8,128)S(1)} fusion(f32[1024]{0:T(1024)S(1)} %bitcast.296, f32[512]{0:T(512)S(1)} %bitcast.322, f32[1024]{0:T(1024)S(1)} %bitcast.298, f32[512]{0:T(512)S(1)} %bitcast.320, f32[1024]{0:T(1024)S(1)} %bitcast.294, f32[512]{0:T(512)S(1)} %bitcast.318, bf16[128,4096]{1,0:T(8,128)(2,1)} %get-tuple-element.940, ...), kind=kOutput, calls=%fused_computation.62.clone.1 | convolution fusion | flops 140509184 | bytes 542724 | tf_op jit(solution)/shard_map/while/body/eval_jaxpr/dot_general | solution.py:36
  454.7 9.6 %fusion.105 = f32[512,128]{0,1:T(8,128)S(1)} fusion(f32[1024]{0:T(1024)S(1)} %bitcast.297, f32[512]{0:T(512)S(1)} %bitcast.323, f32[1024]{0:T(1024)S(1)} %bitcast.299, f32[512]{0:T(512)S(1)} %bitcast.321, f32[1024]{0:T(1024)S(1)} %bitcast.295, f32[512]{0:T(512)S(1)} %bitcast.319, bf16[128,4096]{1,0:T(8,128)(2,1)} %get-tuple-element.940, ...), kind=kOutput, calls=%fused_computation.61.clone.1 | convolution fusion | flops 140509184 | bytes 542724 | tf_op jit(solution)/shard_map/while/body/eval_jaxpr/dot_general | solution.py:35
  464.5 9.7 %fusion.104 = f32[512,128]{0,1:T(8,128)S(1)} fusion(f32[1024]{0:T(1024)S(1)} %bitcast.296, f32[512]{0:T(512)S(1)} %bitcast.322, f32[1024]{0:T(1024)S(1)} %bitcast.298, f32[512]{0:T(512)S(1)} %bitcast.320, f32[1024]{0:T(1024)S(1)} %bitcast.294, f32[512]{0:T(512)S(1)} %bitcast.318, bf16[128,4096]{1,0:T(8,128)(2,1)} %get-tuple-element.940, ...), kind=kOutput, calls=%fused_computation.62.clone.1 | convolution fusion | flops 140509184 | bytes 542724 | tf_op jit(solution)/shard_map/while/body/eval_jaxpr/dot_general | solution.py:36
  474.2 9.6 %fusion.105 = f32[512,128]{0,1:T(8,128)S(1)} fusion(f32[1024]{0:T(1024)S(1)} %bitcast.297, f32[512]{0:T(512)S(1)} %bitcast.323, f32[1024]{0:T(1024)S(1)} %bitcast.299, f32[512]{0:T(512)S(1)} %bitcast.321, f32[1024]{0:T(1024)S(1)} %bitcast.295, f32[512]{0:T(512)S(1)} %bitcast.319, bf16[128,4096]{1,0:T(8,128)(2,1)} %get-tuple-element.940, ...), kind=kOutput, calls=%fused_computation.61.clone.1 | convolution fusion | flops 140509184 | bytes 542724 | tf_op jit(solution)/shard_map/while/body/eval_jaxpr/dot_general | solution.py:35
  484.1 9.7 %fusion.104 = f32[512,128]{0,1:T(8,128)S(1)} fusion(f32[1024]{0:T(1024)S(1)} %bitcast.296, f32[512]{0:T(512)S(1)} %bitcast.322, f32[1024]{0:T(1024)S(1)} %bitcast.298, f32[512]{0:T(512)S(1)} %bitcast.320, f32[1024]{0:T(1024)S(1)} %bitcast.294, f32[512]{0:T(512)S(1)} %bitcast.318, bf16[128,4096]{1,0:T(8,128)(2,1)} %get-tuple-element.940, ...), kind=kOutput, calls=%fused_computation.62.clone.1 | convolution fusion | flops 140509184 | bytes 542724 | tf_op jit(solution)/shard_map/while/body/eval_jaxpr/dot_general | solution.py:36
  493.8 9.6 %fusion.105 = f32[512,128]{0,1:T(8,128)S(1)} fusion(f32[1024]{0:T(1024)S(1)} %bitcast.297, f32[512]{0:T(512)S(1)} %bitcast.323, f32[1024]{0:T(1024)S(1)} %bitcast.299, f32[512]{0:T(512)S(1)} %bitcast.321, f32[1024]{0:T(1024)S(1)} %bitcast.295, f32[512]{0:T(512)S(1)} %bitcast.319, bf16[128,4096]{1,0:T(8,128)(2,1)} %get-tuple-element.940, ...), kind=kOutput, calls=%fused_computation.61.clone.1 | convolution fusion | flops 140509184 | bytes 542724 | tf_op jit(solution)/shard_map/while/body/eval_jaxpr/dot_general | solution.py:35
  503.6 9.7 %fusion.104 = f32[512,128]{0,1:T(8,128)S(1)} fusion(f32[1024]{0:T(1024)S(1)} %bitcast.296, f32[512]{0:T(512)S(1)} %bitcast.322, f32[1024]{0:T(1024)S(1)} %bitcast.298, f32[512]{0:T(512)S(1)} %bitcast.320, f32[1024]{0:T(1024)S(1)} %bitcast.294, f32[512]{0:T(512)S(1)} %bitcast.318, bf16[128,4096]{1,0:T(8,128)(2,1)} %get-tuple-element.940, ...), kind=kOutput, calls=%fused_computation.62.clone.1 | convolution fusion | flops 140509184 | bytes 542724 | tf_op jit(solution)/shard_map/while/body/eval_jaxpr/dot_general | solution.py:36
  513.3 9.6 %fusion.105 = f32[512,128]{0,1:T(8,128)S(1)} fusion(f32[1024]{0:T(1024)S(1)} %bitcast.297, f32[512]{0:T(512)S(1)} %bitcast.323, f32[1024]{0:T(1024)S(1)} %bitcast.299, f32[512]{0:T(512)S(1)} %bitcast.321, f32[1024]{0:T(1024)S(1)} %bitcast.295, f32[512]{0:T(512)S(1)} %bitcast.319, bf16[128,4096]{1,0:T(8,128)(2,1)} %get-tuple-element.940, ...), kind=kOutput, calls=%fused_computation.61.clone.1 | convolution fusion | flops 140509184 | bytes 542724 | tf_op jit(solution)/shard_map/while/body/eval_jaxpr/dot_general | solution.py:35
  523.1 0.8 copy.56
  524.0 71.3 %all-reduce.2.cloned.1.call-done = f32[512,128]{1,0:T(8,128)} async-done(((f32[512,128]{1,0:T(8,128)}), f32[512,128]{1,0:T(8,128)}) %all-reduce.2.cloned.1.call-update) | async-done | bytes 262160 | tf_op jit(solution)/shard_map/psum | solution.py:111
  595.3 1.1 broadcast_multiply_fusion
  596.5 7.5 %collective-permute-start.1 = (f32[8,128]{1,0:T(8,128)S(1)}, f32[8,128]{1,0:T(8,128)S(1)}, u32[]{:S(2)}, u32[]{:S(2)}) collective-permute-start(f32[8,128]{1,0:T(8,128)S(1)} %get-tuple-element.560), channel_id=1, source_target_pairs={{8,0},{16,8},{24,16},{32,24},{40,32},{48,40},{56,48},{64,56},{72,6... | collective-permute-start | bytes 12296 | tf_op jit(solution)/shard_map/ppermute | solution.py:20
  604.0 4.2 collective-permute-start
  619.2 1.6 multiply_add_fusion
  (173 shorter events, 14.1 us)
Async XLA Ops:
  6.5 190.0 %all-gather.9.cloned.1.call-start = ((), (), s32[]{:S(2)}) async-start(), calls=%async_computation | async-start | bytes 1081344 | tf_op jit(solution)/shard_map/all_gather | solution.py:108
  17.7 5.0 copy-start.6
  17.7 5.0 copy-start.7
  17.7 5.0 copy-start.8
  17.7 5.1 copy-start.5
  23.6 251.7 %all-gather.11.cloned.1.call-start = ((), (), s32[]{:S(2)}) async-start(), calls=%async_computation.1 | async-start | bytes 1081344 | tf_op jit(solution)/shard_map/all_gather | solution.py:108
  26.8 326.6 %all-gather.13.cloned.1.call-start = ((), (), s32[]{:S(2)}) async-start(), calls=%async_computation.2 | async-start | bytes 1081344 | tf_op jit(solution)/shard_map/all_gather | solution.py:108
  32.7 4.5 copy-start.4
  33.0 163.5 %copy-start = (bf16[3,512]{1,0:T(4,128)(2,1)S(1)}, bf16[3,512]{1,0:T(4,128)(2,1)}, u32[]{:S(2)}) copy-start(bf16[3,512]{1,0:T(4,128)(2,1)} %param.20) | copy-start | bytes 9220
  33.9 397.9 %all-gather.15.cloned.1.call-start = ((), (), s32[]{:S(2)}) async-start(), calls=%async_computation.3 | async-start | bytes 1081344 | tf_op jit(solution)/shard_map/all_gather | solution.py:108
  37.2 558.2 %all-reduce.2.cloned.1.call-start = ((), (), s32[]{:S(2)}) async-start(), calls=%async_computation.4 | async-start | bytes 524288 | tf_op jit(solution)/shard_map/psum | solution.py:111
  431.8 92.1 %copy-start.9 = (f32[512]{0:T(512)S(1)}, f32[512]{0:T(512)}, u32[]{:S(2)}) copy-start(f32[512]{0:T(512)} %param.21) | copy-start | bytes 6148
  431.8 92.1 %copy-start.3 = (f32[8,512]{1,0:T(8,128)S(1)}, f32[8,512]{1,0:T(8,128)}, u32[]{:S(2)}) copy-start(f32[8,512]{1,0:T(8,128)} %param.30) | copy-start | bytes 49156
  523.1 85.2 %copy-start.2 = (s32[8]{0:T(128)S(1)}, s32[8]{0:T(128)}, u32[]{:S(2)}) copy-start(s32[8]{0:T(128)} %param.31) | copy-start | bytes 100
  595.3 23.9 %copy-start.1 = (f32[512,128]{1,0:T(8,128)S(1)}, f32[512,128]{1,0:T(8,128)}, u32[]{:S(2)}) copy-start(f32[512,128]{1,0:T(8,128)} %all-reduce.2.cloned.1.call-done) | copy-start | bytes 786436
  596.5 22.7 %collective-permute-start.1 = (f32[8,128]{1,0:T(8,128)S(1)}, f32[8,128]{1,0:T(8,128)S(1)}, u32[]{:S(2)}, u32[]{:S(2)}) collective-permute-start(f32[8,128]{1,0:T(8,128)S(1)} %get-tuple-element.560), channel_id=1, source_target_pairs={{8,0},{16,8},{24,16},{32,24},{40,32},{48,40},{56,48},{64,56},{72,6... | collective-permute-start | bytes 12296 | tf_op jit(solution)/shard_map/ppermute | solution.py:20
  604.0 15.2 %collective-permute-start = (f32[8,128]{1,0:T(8,128)S(1)}, f32[8,128]{1,0:T(8,128)S(1)}, u32[]{:S(2)}, u32[]{:S(2)}) collective-permute-start(f32[8,128]{1,0:T(8,128)S(1)} %get-tuple-element.559), channel_id=1, source_target_pairs={{0,8},{8,16},{16,24},{24,32},{32,40},{40,48},{48,56},{56,64},{64,7... | collective-permute-start | bytes 12296 | tf_op jit(solution)/shard_map/ppermute | solution.py:17
Sparse Core Ops, SparseCore 0:
  23.7 76.4 all-gather.8
  102.7 70.0 all-gather.10
  175.4 69.8 all-gather.12
  247.7 69.9 all-gather.14
  524.1 71.2 all-reduce.1
where the time goes:
time: 635 us; the launch traced here: 628 us
  matrix products  309 us (49%)
  blocking collectives  159 us (25%)
  waiting for transfers between devices  71.5 us (11%)
  local copies, waits for them, and re-layouts  28.2 us (4%)
  between operations  24.2 us (4%)
  loops' own time  15.1 us (2%)
  starting transfers between devices  11.9 us (2%)
  other arithmetic  8.44 us (1%)
    all_gather x4, blocking collectives, per_device(): lax.all_gather(src_points[section], 'tgt', axis=1, tiled=True)  159 us
    dot_general x16, matrix products, kernel_terms(): lax.dot_general(kernel_im, density, dims, preferred_element_type=jnp.floa...  155 us
    dot_general x16, matrix products, kernel_terms(): lax.dot_general(kernel_re, density, dims, preferred_element_type=jnp.floa...  154 us
    psum x1, waiting for transfers between devices, per_device(): total = lax.psum(partial_value, 'src')  71.3 us
    another operation x4, loops' own time, add_kernel(): return lax.fori_loop(0, width // block_size, step_fn, carried)  15.1 us
    gather x12, local copies, waits for them, and re-layouts, block_density(): scaled = basis_rows[basis_index] * weights_ctrl[control_index]  14.7 us
  transfers between devices with their start and end apart: 7, of which 1 were waited for; matrix products, arithmetic and copies ran while one was open for 39% of the time, Pallas kernels for 0%

commit v1 on v0

--- a/solution.py
+++ b/solution.py
@@ -7,6 +7,11 @@
 HALO = 8
 WAVE = 8.0
 SMOOTH = 0.0025
+
+
+def add_all(array, name):
+    parts = lax.all_gather(array, name)
+    return jnp.sum(parts, axis=0)
 
 
 def extended(block, sides, width):
@@ -108,7 +113,7 @@
             lax.all_gather(density, "tgt", axis=1, tiled=True),
         )
         partial_value = add_kernel(partial_value, tgt_points, geometry, gathered)
-    total = lax.psum(partial_value, "src")
+    total = add_all(partial_value, "src")
     source_count = rounds * src_weight.shape[1] * lax.axis_size("tgt") * lax.axis_size("src")
     scale = jnp.float32(1.0 / math.sqrt(source_count))
     potential = total * scale * tgt_weight[:, None]

time: 635 us -> 590 us (0.929)
  waiting for transfers between devices: 71.5 us -> 36.7 us
  loops' own time: 15.1 us -> 2.51 us
    psum x1 -> x0, waiting for transfers between devices: 71.3 us -> none  [per_device(): total = lax.psum(partial_value, 'src')]
    all_gather x0 -> x1, waiting for transfers between devices: none -> 36.5 us  [add_all(): parts = lax.all_gather(array, name)]
    another operation x4, loops' own time: 15.1 us -> 2.51 us  [add_kernel(): return lax.fori_loop(0, width // block_size, step_fn, carried)]
  transfers between devices with their start and end apart: 7 -> 7, of which waited for: 1 -> 1; matrix products, arithmetic and copies ran while one was open for 39% -> 42% of each run, Pallas kernels for 0% -> 0%
where the time goes in v1:
time: 590 us; the launch traced here: 583 us
  matrix products  309 us (52%)
  blocking collectives  159 us (27%)
  waiting for transfers between devices  36.7 us (6%)
  local copies, waits for them, and re-layouts  32.1 us (5%)
  between operations  23.8 us (4%)
  starting transfers between devices  12 us (2%)
  other arithmetic  7.1 us (1%)
    all_gather x4, blocking collectives, per_device(): lax.all_gather(src_points[section], 'tgt', axis=1, tiled=True)  159 us
    dot_general x16, matrix products, kernel_terms(): lax.dot_general(kernel_im, density, dims, preferred_element_type=jnp.floa...  155 us
    dot_general x16, matrix products, kernel_terms(): lax.dot_general(kernel_re, density, dims, preferred_element_type=jnp.floa...  154 us
    all_gather x1, waiting for transfers between devices, add_all(): parts = lax.all_gather(array, name)  36.5 us
    gather x12, local copies, waits for them, and re-layouts, block_density(): scaled = basis_rows[basis_index] * weights_ctrl[control_index]  14.7 us
  transfers between devices with their start and end apart: 7, of which 1 were waited for; matrix products, arithmetic and copies ran while one was open for 42% of the time, Pallas kernels for 0%

profile of v1, /device:TPU:1, one launch (start us, length us, event | category | flops | bytes accessed | tf_op | source)
XLA Modules:
  0.0 582.6 jit_solution(13544731527268991876)
XLA Ops:
  6.5 0.7 slice_bitcast_fusion
  7.3 0.8 fusion.49
  8.1 0.7 gather_fusion.5
  9.6 0.8 slice_bitcast_fusion.5
  10.4 1.2 gather_fusion.4
  11.6 1.2 gather_fusion.2
  13.6 1.2 gather_fusion
  15.2 1.2 gather_fusion.20
  16.5 1.2 gather_fusion.18
  17.7 1.2 gather_fusion.22
  19.0 1.2 gather_fusion.10
  20.2 1.2 gather_fusion.8
  21.4 1.2 gather_fusion.6
  26.9 0.7 gather_fusion.15
  27.6 0.7 gather_fusion.13
  28.3 1.2 gather_fusion.14
  29.6 1.2 gather_fusion.12
  30.8 0.7 gather_fusion.17
  31.5 1.2 gather_fusion.16
  37.3 46.2 %all-gather = bf16[1,3,4096]{2,1,0:T(4,128)(2,1)S(1)} all-gather(bf16[1,3,128]{2,1,0:T(4,128)(2,1)S(1)} %copy.64), channel_id=2, replica_groups=mesh['tgt'=32,'src'=8] {'tgt'}, dimensions={2}, use_global_device_ids=true | all-gather | bytes 25344 | tf_op jit(solution)/shard_map/all_gather | solution.py:112
  83.5 36.7 %all-gather.1 = bf16[1,3,4096]{2,1,0:T(4,128)(2,1)S(1)} all-gather(bf16[1,3,128]{2,1,0:T(4,128)(2,1)S(1)} %copy.65), channel_id=3, replica_groups=mesh['tgt'=32,'src'=8] {'tgt'}, dimensions={2}, use_global_device_ids=true | all-gather | bytes 25344 | tf_op jit(solution)/shard_map/all_gather | solution.py:112
  120.2 39.6 %all-gather.2 = bf16[1,3,4096]{2,1,0:T(4,128)(2,1)S(1)} all-gather(bf16[1,3,128]{2,1,0:T(4,128)(2,1)S(1)} %copy.66), channel_id=4, replica_groups=mesh['tgt'=32,'src'=8] {'tgt'}, dimensions={2}, use_global_device_ids=true | all-gather | bytes 25344 | tf_op jit(solution)/shard_map/all_gather | solution.py:112
  159.8 36.7 %all-gather.3 = bf16[1,3,4096]{2,1,0:T(4,128)(2,1)S(1)} all-gather(bf16[1,3,128]{2,1,0:T(4,128)(2,1)S(1)} %copy.67), channel_id=5, replica_groups=mesh['tgt'=32,'src'=8] {'tgt'}, dimensions={2}, use_global_device_ids=true | all-gather | bytes 25344 | tf_op jit(solution)/shard_map/all_gather | solution.py:112
  196.5 78.8 %while.56 = (s32[]{:T(128)}, f32[512,128]{0,1:T(8,128)S(1)}, bf16[3,512]{1,0:T(4,128)(2,1)S(1)}, bf16[3,4096]{1,0:T(4,128)(2,1)S(1)}, bf16[128,4096]{1,0:T(8,128...) while((s32[]{:T(128)}, f32[512,128]{0,1:T(8,128)S(1)}, bf16[3,512]{1,0:T(4,128)(2,1)S(1)}, ...), condition=%wide.region_3.4_spmd.clone, body=%wide.region_2.3_spmd.clone.sunk | while | flops 281283584 | bytes 2713769 | solution.py:80
  196.7 9.7 %fusion.110 = f32[512,128]{0,1:T(8,128)S(1)} fusion(f32[1024]{0:T(1024)S(1)} %bitcast.284, f32[512]{0:T(512)S(1)} %bitcast.310, f32[1024]{0:T(1024)S(1)} %bitcast.286, f32[512]{0:T(512)S(1)} %bitcast.308, f32[1024]{0:T(1024)S(1)} %bitcast.282, f32[512]{0:T(512)S(1)} %bitcast.306, bf16[128,4096]{1,0:T(8,128)(2,1)} %get-tuple-element.879, ...), kind=kOutput, calls=%fused_computation.79.clone.1 | convolution fusion | flops 140509184 | bytes 542724 | tf_op jit(solution)/shard_map/while/body/eval_jaxpr/dot_general | solution.py:41
  206.4 9.6 %fusion.111 = f32[512,128]{0,1:T(8,128)S(1)} fusion(f32[1024]{0:T(1024)S(1)} %bitcast.285, f32[512]{0:T(512)S(1)} %bitcast.311, f32[1024]{0:T(1024)S(1)} %bitcast.287, f32[512]{0:T(512)S(1)} %bitcast.309, f32[1024]{0:T(1024)S(1)} %bitcast.283, f32[512]{0:T(512)S(1)} %bitcast.307, bf16[128,4096]{1,0:T(8,128)(2,1)} %get-tuple-element.879, ...), kind=kOutput, calls=%fused_computation.78.clone.1 | convolution fusion | flops 140509184 | bytes 542724 | tf_op jit(solution)/shard_map/while/body/eval_jaxpr/dot_general | solution.py:40
  216.3 9.7 %fusion.110 = f32[512,128]{0,1:T(8,128)S(1)} fusion(f32[1024]{0:T(1024)S(1)} %bitcast.284, f32[512]{0:T(512)S(1)} %bitcast.310, f32[1024]{0:T(1024)S(1)} %bitcast.286, f32[512]{0:T(512)S(1)} %bitcast.308, f32[1024]{0:T(1024)S(1)} %bitcast.282, f32[512]{0:T(512)S(1)} %bitcast.306, bf16[128,4096]{1,0:T(8,128)(2,1)} %get-tuple-element.879, ...), kind=kOutput, calls=%fused_computation.79.clone.1 | convolution fusion | flops 140509184 | bytes 542724 | tf_op jit(solution)/shard_map/while/body/eval_jaxpr/dot_general | solution.py:41
  226.0 9.6 %fusion.111 = f32[512,128]{0,1:T(8,128)S(1)} fusion(f32[1024]{0:T(1024)S(1)} %bitcast.285, f32[512]{0:T(512)S(1)} %bitcast.311, f32[1024]{0:T(1024)S(1)} %bitcast.287, f32[512]{0:T(512)S(1)} %bitcast.309, f32[1024]{0:T(1024)S(1)} %bitcast.283, f32[512]{0:T(512)S(1)} %bitcast.307, bf16[128,4096]{1,0:T(8,128)(2,1)} %get-tuple-element.879, ...), kind=kOutput, calls=%fused_computation.78.clone.1 | convolution fusion | flops 140509184 | bytes 542724 | tf_op jit(solution)/shard_map/while/body/eval_jaxpr/dot_general | solution.py:40
  235.8 9.7 %fusion.110 = f32[512,128]{0,1:T(8,128)S(1)} fusion(f32[1024]{0:T(1024)S(1)} %bitcast.284, f32[512]{0:T(512)S(1)} %bitcast.310, f32[1024]{0:T(1024)S(1)} %bitcast.286, f32[512]{0:T(512)S(1)} %bitcast.308, f32[1024]{0:T(1024)S(1)} %bitcast.282, f32[512]{0:T(512)S(1)} %bitcast.306, bf16[128,4096]{1,0:T(8,128)(2,1)} %get-tuple-element.879, ...), kind=kOutput, calls=%fused_computation.79.clone.1 | convolution fusion | flops 140509184 | bytes 542724 | tf_op jit(solution)/shard_map/while/body/eval_jaxpr/dot_general | solution.py:41
  245.5 9.6 %fusion.111 = f32[512,128]{0,1:T(8,128)S(1)} fusion(f32[1024]{0:T(1024)S(1)} %bitcast.285, f32[512]{0:T(512)S(1)} %bitcast.311, f32[1024]{0:T(1024)S(1)} %bitcast.287, f32[512]{0:T(512)S(1)} %bitcast.309, f32[1024]{0:T(1024)S(1)} %bitcast.283, f32[512]{0:T(512)S(1)} %bitcast.307, bf16[128,4096]{1,0:T(8,128)(2,1)} %get-tuple-element.879, ...), kind=kOutput, calls=%fused_computation.78.clone.1 | convolution fusion | flops 140509184 | bytes 542724 | tf_op jit(solution)/shard_map/while/body/eval_jaxpr/dot_general | solution.py:40
  255.4 9.7 %fusion.110 = f32[512,128]{0,1:T(8,128)S(1)} fusion(f32[1024]{0:T(1024)S(1)} %bitcast.284, f32[512]{0:T(512)S(1)} %bitcast.310, f32[1024]{0:T(1024)S(1)} %bitcast.286, f32[512]{0:T(512)S(1)} %bitcast.308, f32[1024]{0:T(1024)S(1)} %bitcast.282, f32[512]{0:T(512)S(1)} %bitcast.306, bf16[128,4096]{1,0:T(8,128)(2,1)} %get-tuple-element.879, ...), kind=kOutput, calls=%fused_computation.79.clone.1 | convolution fusion | flops 140509184 | bytes 542724 | tf_op jit(solution)/shard_map/while/body/eval_jaxpr/dot_general | solution.py:41
  265.1 9.6 %fusion.111 = f32[512,128]{0,1:T(8,128)S(1)} fusion(f32[1024]{0:T(1024)S(1)} %bitcast.285, f32[512]{0:T(512)S(1)} %bitcast.311, f32[1024]{0:T(1024)S(1)} %bitcast.287, f32[512]{0:T(512)S(1)} %bitcast.309, f32[1024]{0:T(1024)S(1)} %bitcast.283, f32[512]{0:T(512)S(1)} %bitcast.307, bf16[128,4096]{1,0:T(8,128)(2,1)} %get-tuple-element.879, ...), kind=kOutput, calls=%fused_computation.78.clone.1 | convolution fusion | flops 140509184 | bytes 542724 | tf_op jit(solution)/shard_map/while/body/eval_jaxpr/dot_general | solution.py:40
  275.3 78.1 %while.53 = (s32[]{:T(128)}, f32[512,128]{0,1:T(8,128)S(1)}, bf16[3,512]{1,0:T(4,128)(2,1)S(1)}, bf16[3,4096]{1,0:T(4,128)(2,1)S(1)}, bf16[128,4096]{1,0:T(8,128...) while((s32[]{:T(128)}, f32[512,128]{0,1:T(8,128)S(1)}, bf16[3,512]{1,0:T(4,128)(2,1)S(1)}, ...), condition=%wide.region_7.8_spmd, body=%wide.region_6.7_spmd.sunk | while | flops 281218048 | bytes 2713759 | solution.py:80
  275.4 9.7 %fusion.92 = f32[512,128]{0,1:T(8,128)S(1)} fusion(f32[1024]{0:T(1024)S(1)} %bitcast.290, f32[512]{0:T(512)S(1)} %bitcast.316, f32[1024]{0:T(1024)S(1)} %bitcast.292, f32[512]{0:T(512)S(1)} %bitcast.314, f32[1024]{0:T(1024)S(1)} %bitcast.288, f32[512]{0:T(512)S(1)} %bitcast.312, bf16[128,4096]{1,0:T(8,128)(2,1)} %get-tuple-element.906, ...), kind=kOutput, calls=%fused_computation.28.clone.1 | convolution fusion | flops 140509184 | bytes 542724 | tf_op jit(solution)/shard_map/while/body/eval_jaxpr/dot_general | solution.py:41
  285.1 9.6 %fusion.93 = f32[512,128]{0,1:T(8,128)S(1)} fusion(f32[1024]{0:T(1024)S(1)} %bitcast.291, f32[512]{0:T(512)S(1)} %bitcast.317, f32[1024]{0:T(1024)S(1)} %bitcast.293, f32[512]{0:T(512)S(1)} %bitcast.315, f32[1024]{0:T(1024)S(1)} %bitcast.289, f32[512]{0:T(512)S(1)} %bitcast.313, bf16[128,4096]{1,0:T(8,128)(2,1)} %get-tuple-element.906, ...), kind=kOutput, calls=%fused_computation.27.clone.1 | convolution fusion | flops 140509184 | bytes 542724 | tf_op jit(solution)/shard_map/while/body/eval_jaxpr/dot_general | solution.py:40
  294.9 9.7 %fusion.92 = f32[512,128]{0,1:T(8,128)S(1)} fusion(f32[1024]{0:T(1024)S(1)} %bitcast.290, f32[512]{0:T(512)S(1)} %bitcast.316, f32[1024]{0:T(1024)S(1)} %bitcast.292, f32[512]{0:T(512)S(1)} %bitcast.314, f32[1024]{0:T(1024)S(1)} %bitcast.288, f32[512]{0:T(512)S(1)} %bitcast.312, bf16[128,4096]{1,0:T(8,128)(2,1)} %get-tuple-element.906, ...), kind=kOutput, calls=%fused_computation.28.clone.1 | convolution fusion | flops 140509184 | bytes 542724 | tf_op jit(solution)/shard_map/while/body/eval_jaxpr/dot_general | solution.py:41
  304.6 9.6 %fusion.93 = f32[512,128]{0,1:T(8,128)S(1)} fusion(f32[1024]{0:T(1024)S(1)} %bitcast.291, f32[512]{0:T(512)S(1)} %bitcast.317, f32[1024]{0:T(1024)S(1)} %bitcast.293, f32[512]{0:T(512)S(1)} %bitcast.315, f32[1024]{0:T(1024)S(1)} %bitcast.289, f32[512]{0:T(512)S(1)} %bitcast.313, bf16[128,4096]{1,0:T(8,128)(2,1)} %get-tuple-element.906, ...), kind=kOutput, calls=%fused_computation.27.clone.1 | convolution fusion | flops 140509184 | bytes 542724 | tf_op jit(solution)/shard_map/while/body/eval_jaxpr/dot_general | solution.py:40
  314.4 9.7 %fusion.92 = f32[512,128]{0,1:T(8,128)S(1)} fusion(f32[1024]{0:T(1024)S(1)} %bitcast.290, f32[512]{0:T(512)S(1)} %bitcast.316, f32[1024]{0:T(1024)S(1)} %bitcast.292, f32[512]{0:T(512)S(1)} %bitcast.314, f32[1024]{0:T(1024)S(1)} %bitcast.288, f32[512]{0:T(512)S(1)} %bitcast.312, bf16[128,4096]{1,0:T(8,128)(2,1)} %get-tuple-element.906, ...), kind=kOutput, calls=%fused_computation.28.clone.1 | convolution fusion | flops 140509184 | bytes 542724 | tf_op jit(solution)/shard_map/while/body/eval_jaxpr/dot_general | solution.py:41
  324.1 9.6 %fusion.93 = f32[512,128]{0,1:T(8,128)S(1)} fusion(f32[1024]{0:T(1024)S(1)} %bitcast.291, f32[512]{0:T(512)S(1)} %bitcast.317, f32[1024]{0:T(1024)S(1)} %bitcast.293, f32[512]{0:T(512)S(1)} %bitcast.315, f32[1024]{0:T(1024)S(1)} %bitcast.289, f32[512]{0:T(512)S(1)} %bitcast.313, bf16[128,4096]{1,0:T(8,128)(2,1)} %get-tuple-element.906, ...), kind=kOutput, calls=%fused_computation.27.clone.1 | convolution fusion | flops 140509184 | bytes 542724 | tf_op jit(solution)/shard_map/while/body/eval_jaxpr/dot_general | solution.py:40
  334.0 9.7 %fusion.92 = f32[512,128]{0,1:T(8,128)S(1)} fusion(f32[1024]{0:T(1024)S(1)} %bitcast.290, f32[512]{0:T(512)S(1)} %bitcast.316, f32[1024]{0:T(1024)S(1)} %bitcast.292, f32[512]{0:T(512)S(1)} %bitcast.314, f32[1024]{0:T(1024)S(1)} %bitcast.288, f32[512]{0:T(512)S(1)} %bitcast.312, bf16[128,4096]{1,0:T(8,128)(2,1)} %get-tuple-element.906, ...), kind=kOutput, calls=%fused_computation.28.clone.1 | convolution fusion | flops 140509184 | bytes 542724 | tf_op jit(solution)/shard_map/while/body/eval_jaxpr/dot_general | solution.py:41
  343.7 9.6 %fusion.93 = f32[512,128]{0,1:T(8,128)S(1)} fusion(f32[1024]{0:T(1024)S(1)} %bitcast.291, f32[512]{0:T(512)S(1)} %bitcast.317, f32[1024]{0:T(1024)S(1)} %bitcast.293, f32[512]{0:T(512)S(1)} %bitcast.315, f32[1024]{0:T(1024)S(1)} %bitcast.289, f32[512]{0:T(512)S(1)} %bitcast.313, bf16[128,4096]{1,0:T(8,128)(2,1)} %get-tuple-element.906, ...), kind=kOutput, calls=%fused_computation.27.clone.1 | convolution fusion | flops 140509184 | bytes 542724 | tf_op jit(solution)/shard_map/while/body/eval_jaxpr/dot_general | solution.py:40
  353.5 78.3 %while.54 = (s32[]{:T(128)}, f32[512,128]{0,1:T(8,128)S(1)}, bf16[3,512]{1,0:T(4,128)(2,1)S(1)}, bf16[3,4096]{1,0:T(4,128)(2,1)S(1)}, bf16[128,4096]{1,0:T(8,128...) while((s32[]{:T(128)}, f32[512,128]{0,1:T(8,128)S(1)}, bf16[3,512]{1,0:T(4,128)(2,1)S(1)}, ...), condition=%wide.region_11.12_spmd, body=%wide.region_10.11_spmd.sunk | while | flops 281218048 | bytes 2713759 | solution.py:80
  353.7 9.7 %fusion.98 = f32[512,128]{0,1:T(8,128)S(1)} fusion(f32[1024]{0:T(1024)S(1)} %bitcast.296, f32[512]{0:T(512)S(1)} %bitcast.322, f32[1024]{0:T(1024)S(1)} %bitcast.298, f32[512]{0:T(512)S(1)} %bitcast.320, f32[1024]{0:T(1024)S(1)} %bitcast.294, f32[512]{0:T(512)S(1)} %bitcast.318, bf16[128,4096]{1,0:T(8,128)(2,1)} %get-tuple-element.933, ...), kind=kOutput, calls=%fused_computation.45.clone.1 | convolution fusion | flops 140509184 | bytes 542724 | tf_op jit(solution)/shard_map/while/body/eval_jaxpr/dot_general | solution.py:41
  363.4 9.6 %fusion.99 = f32[512,128]{0,1:T(8,128)S(1)} fusion(f32[1024]{0:T(1024)S(1)} %bitcast.297, f32[512]{0:T(512)S(1)} %bitcast.323, f32[1024]{0:T(1024)S(1)} %bitcast.299, f32[512]{0:T(512)S(1)} %bitcast.321, f32[1024]{0:T(1024)S(1)} %bitcast.295, f32[512]{0:T(512)S(1)} %bitcast.319, bf16[128,4096]{1,0:T(8,128)(2,1)} %get-tuple-element.933, ...), kind=kOutput, calls=%fused_computation.44.clone.1 | convolution fusion | flops 140509184 | bytes 542724 | tf_op jit(solution)/shard_map/while/body/eval_jaxpr/dot_general | solution.py:40
  373.2 9.7 %fusion.98 = f32[512,128]{0,1:T(8,128)S(1)} fusion(f32[1024]{0:T(1024)S(1)} %bitcast.296, f32[512]{0:T(512)S(1)} %bitcast.322, f32[1024]{0:T(1024)S(1)} %bitcast.298, f32[512]{0:T(512)S(1)} %bitcast.320, f32[1024]{0:T(1024)S(1)} %bitcast.294, f32[512]{0:T(512)S(1)} %bitcast.318, bf16[128,4096]{1,0:T(8,128)(2,1)} %get-tuple-element.933, ...), kind=kOutput, calls=%fused_computation.45.clone.1 | convolution fusion | flops 140509184 | bytes 542724 | tf_op jit(solution)/shard_map/while/body/eval_jaxpr/dot_general | solution.py:41
  382.9 9.6 %fusion.99 = f32[512,128]{0,1:T(8,128)S(1)} fusion(f32[1024]{0:T(1024)S(1)} %bitcast.297, f32[512]{0:T(512)S(1)} %bitcast.323, f32[1024]{0:T(1024)S(1)} %bitcast.299, f32[512]{0:T(512)S(1)} %bitcast.321, f32[1024]{0:T(1024)S(1)} %bitcast.295, f32[512]{0:T(512)S(1)} %bitcast.319, bf16[128,4096]{1,0:T(8,128)(2,1)} %get-tuple-element.933, ...), kind=kOutput, calls=%fused_computation.44.clone.1 | convolution fusion | flops 140509184 | bytes 542724 | tf_op jit(solution)/shard_map/while/body/eval_jaxpr/dot_general | solution.py:40
  392.8 9.7 %fusion.98 = f32[512,128]{0,1:T(8,128)S(1)} fusion(f32[1024]{0:T(1024)S(1)} %bitcast.296, f32[512]{0:T(512)S(1)} %bitcast.322, f32[1024]{0:T(1024)S(1)} %bitcast.298, f32[512]{0:T(512)S(1)} %bitcast.320, f32[1024]{0:T(1024)S(1)} %bitcast.294, f32[512]{0:T(512)S(1)} %bitcast.318, bf16[128,4096]{1,0:T(8,128)(2,1)} %get-tuple-element.933, ...), kind=kOutput, calls=%fused_computation.45.clone.1 | convolution fusion | flops 140509184 | bytes 542724 | tf_op jit(solution)/shard_map/while/body/eval_jaxpr/dot_general | solution.py:41
  402.5 9.6 %fusion.99 = f32[512,128]{0,1:T(8,128)S(1)} fusion(f32[1024]{0:T(1024)S(1)} %bitcast.297, f32[512]{0:T(512)S(1)} %bitcast.323, f32[1024]{0:T(1024)S(1)} %bitcast.299, f32[512]{0:T(512)S(1)} %bitcast.321, f32[1024]{0:T(1024)S(1)} %bitcast.295, f32[512]{0:T(512)S(1)} %bitcast.319, bf16[128,4096]{1,0:T(8,128)(2,1)} %get-tuple-element.933, ...), kind=kOutput, calls=%fused_computation.44.clone.1 | convolution fusion | flops 140509184 | bytes 542724 | tf_op jit(solution)/shard_map/while/body/eval_jaxpr/dot_general | solution.py:40
  412.3 9.7 %fusion.98 = f32[512,128]{0,1:T(8,128)S(1)} fusion(f32[1024]{0:T(1024)S(1)} %bitcast.296, f32[512]{0:T(512)S(1)} %bitcast.322, f32[1024]{0:T(1024)S(1)} %bitcast.298, f32[512]{0:T(512)S(1)} %bitcast.320, f32[1024]{0:T(1024)S(1)} %bitcast.294, f32[512]{0:T(512)S(1)} %bitcast.318, bf16[128,4096]{1,0:T(8,128)(2,1)} %get-tuple-element.933, ...), kind=kOutput, calls=%fused_computation.45.clone.1 | convolution fusion | flops 140509184 | bytes 542724 | tf_op jit(solution)/shard_map/while/body/eval_jaxpr/dot_general | solution.py:41
  422.0 9.6 %fusion.99 = f32[512,128]{0,1:T(8,128)S(1)} fusion(f32[1024]{0:T(1024)S(1)} %bitcast.297, f32[512]{0:T(512)S(1)} %bitcast.323, f32[1024]{0:T(1024)S(1)} %bitcast.299, f32[512]{0:T(512)S(1)} %bitcast.321, f32[1024]{0:T(1024)S(1)} %bitcast.295, f32[512]{0:T(512)S(1)} %bitcast.319, bf16[128,4096]{1,0:T(8,128)(2,1)} %get-tuple-element.933, ...), kind=kOutput, calls=%fused_computation.44.clone.1 | convolution fusion | flops 140509184 | bytes 542724 | tf_op jit(solution)/shard_map/while/body/eval_jaxpr/dot_general | solution.py:40
  431.8 78.7 %while.55 = (s32[]{:T(128)}, f32[512,128]{0,1:T(8,128)S(1)}, bf16[3,512]{1,0:T(4,128)(2,1)S(1)}, bf16[3,4096]{1,0:T(4,128)(2,1)S(1)}, bf16[128,4096]{1,0:T(8,128...) while((s32[]{:T(128)}, f32[512,128]{0,1:T(8,128)S(1)}, bf16[3,512]{1,0:T(4,128)(2,1)S(1)}, ...), condition=%wide.region_15.16_spmd, body=%wide.region_14.15_spmd.sunk | while | flops 281218048 | bytes 2713759 | solution.py:80
  432.3 9.7 %fusion.104 = f32[512,128]{0,1:T(8,128)S(1)} fusion(f32[1024]{0:T(1024)S(1)} %bitcast.302, f32[512]{0:T(512)S(1)} %bitcast.328, f32[1024]{0:T(1024)S(1)} %bitcast.304, f32[512]{0:T(512)S(1)} %bitcast.326, f32[1024]{0:T(1024)S(1)} %bitcast.300, f32[512]{0:T(512)S(1)} %bitcast.324, bf16[128,4096]{1,0:T(8,128)(2,1)} %get-tuple-element.960, ...), kind=kOutput, calls=%fused_computation.62.clone.1 | convolution fusion | flops 140509184 | bytes 542724 | tf_op jit(solution)/shard_map/while/body/eval_jaxpr/dot_general | solution.py:41
  442.0 9.6 %fusion.105 = f32[512,128]{0,1:T(8,128)S(1)} fusion(f32[1024]{0:T(1024)S(1)} %bitcast.303, f32[512]{0:T(512)S(1)} %bitcast.329, f32[1024]{0:T(1024)S(1)} %bitcast.305, f32[512]{0:T(512)S(1)} %bitcast.327, f32[1024]{0:T(1024)S(1)} %bitcast.301, f32[512]{0:T(512)S(1)} %bitcast.325, bf16[128,4096]{1,0:T(8,128)(2,1)} %get-tuple-element.960, ...), kind=kOutput, calls=%fused_computation.61.clone.1 | convolution fusion | flops 140509184 | bytes 542724 | tf_op jit(solution)/shard_map/while/body/eval_jaxpr/dot_general | solution.py:40
  451.8 9.7 %fusion.104 = f32[512,128]{0,1:T(8,128)S(1)} fusion(f32[1024]{0:T(1024)S(1)} %bitcast.302, f32[512]{0:T(512)S(1)} %bitcast.328, f32[1024]{0:T(1024)S(1)} %bitcast.304, f32[512]{0:T(512)S(1)} %bitcast.326, f32[1024]{0:T(1024)S(1)} %bitcast.300, f32[512]{0:T(512)S(1)} %bitcast.324, bf16[128,4096]{1,0:T(8,128)(2,1)} %get-tuple-element.960, ...), kind=kOutput, calls=%fused_computation.62.clone.1 | convolution fusion | flops 140509184 | bytes 542724 | tf_op jit(solution)/shard_map/while/body/eval_jaxpr/dot_general | solution.py:41
  461.5 9.6 %fusion.105 = f32[512,128]{0,1:T(8,128)S(1)} fusion(f32[1024]{0:T(1024)S(1)} %bitcast.303, f32[512]{0:T(512)S(1)} %bitcast.329, f32[1024]{0:T(1024)S(1)} %bitcast.305, f32[512]{0:T(512)S(1)} %bitcast.327, f32[1024]{0:T(1024)S(1)} %bitcast.301, f32[512]{0:T(512)S(1)} %bitcast.325, bf16[128,4096]{1,0:T(8,128)(2,1)} %get-tuple-element.960, ...), kind=kOutput, calls=%fused_computation.61.clone.1 | convolution fusion | flops 140509184 | bytes 542724 | tf_op jit(solution)/shard_map/while/body/eval_jaxpr/dot_general | solution.py:40
  471.3 9.7 %fusion.104 = f32[512,128]{0,1:T(8,128)S(1)} fusion(f32[1024]{0:T(1024)S(1)} %bitcast.302, f32[512]{0:T(512)S(1)} %bitcast.328, f32[1024]{0:T(1024)S(1)} %bitcast.304, f32[512]{0:T(512)S(1)} %bitcast.326, f32[1024]{0:T(1024)S(1)} %bitcast.300, f32[512]{0:T(512)S(1)} %bitcast.324, bf16[128,4096]{1,0:T(8,128)(2,1)} %get-tuple-element.960, ...), kind=kOutput, calls=%fused_computation.62.clone.1 | convolution fusion | flops 140509184 | bytes 542724 | tf_op jit(solution)/shard_map/while/body/eval_jaxpr/dot_general | solution.py:41
  481.0 9.6 %fusion.105 = f32[512,128]{0,1:T(8,128)S(1)} fusion(f32[1024]{0:T(1024)S(1)} %bitcast.303, f32[512]{0:T(512)S(1)} %bitcast.329, f32[1024]{0:T(1024)S(1)} %bitcast.305, f32[512]{0:T(512)S(1)} %bitcast.327, f32[1024]{0:T(1024)S(1)} %bitcast.301, f32[512]{0:T(512)S(1)} %bitcast.325, bf16[128,4096]{1,0:T(8,128)(2,1)} %get-tuple-element.960, ...), kind=kOutput, calls=%fused_computation.61.clone.1 | convolution fusion | flops 140509184 | bytes 542724 | tf_op jit(solution)/shard_map/while/body/eval_jaxpr/dot_general | solution.py:40
  490.9 9.7 %fusion.104 = f32[512,128]{0,1:T(8,128)S(1)} fusion(f32[1024]{0:T(1024)S(1)} %bitcast.302, f32[512]{0:T(512)S(1)} %bitcast.328, f32[1024]{0:T(1024)S(1)} %bitcast.304, f32[512]{0:T(512)S(1)} %bitcast.326, f32[1024]{0:T(1024)S(1)} %bitcast.300, f32[512]{0:T(512)S(1)} %bitcast.324, bf16[128,4096]{1,0:T(8,128)(2,1)} %get-tuple-element.960, ...), kind=kOutput, calls=%fused_computation.62.clone.1 | convolution fusion | flops 140509184 | bytes 542724 | tf_op jit(solution)/shard_map/while/body/eval_jaxpr/dot_general | solution.py:41
  500.6 9.6 %fusion.105 = f32[512,128]{0,1:T(8,128)S(1)} fusion(f32[1024]{0:T(1024)S(1)} %bitcast.303, f32[512]{0:T(512)S(1)} %bitcast.329, f32[1024]{0:T(1024)S(1)} %bitcast.305, f32[512]{0:T(512)S(1)} %bitcast.327, f32[1024]{0:T(1024)S(1)} %bitcast.301, f32[512]{0:T(512)S(1)} %bitcast.325, bf16[128,4096]{1,0:T(8,128)(2,1)} %get-tuple-element.960, ...), kind=kOutput, calls=%fused_computation.61.clone.1 | convolution fusion | flops 140509184 | bytes 542724 | tf_op jit(solution)/shard_map/while/body/eval_jaxpr/dot_general | solution.py:40
  511.3 36.5 %all-gather.19.cloned.1.call-done = f32[4096,128]{0,1:T(8,128)} async-done(((f32[512,128]{0,1:T(8,128)}), f32[4096,128]{0,1:T(8,128)}) %all-gather.19.cloned.1.call-update) | async-done | bytes 2097168 | tf_op jit(solution)/shard_map/all_gather | solution.py:13
  547.8 3.2 copy.68
  551.7 7.6 %collective-permute-start.1 = (f32[8,128]{0,1:T(8,128)S(1)}, f32[8,128]{0,1:T(8,128)S(1)}, u32[]{:S(2)}, u32[]{:S(2)}) collective-permute-start(f32[8,128]{0,1:T(8,128)S(1)} %get-tuple-element.580), channel_id=1, source_target_pairs={{8,0},{16,8},{24,16},{32,24},{40,32},{48,40},{56,48},{64,56},{72,6... | collective-permute-start | bytes 12296 | tf_op jit(solution)/shard_map/ppermute | solution.py:25
  559.3 4.2 collective-permute-start
  575.0 0.8 copy.63
  (175 shorter events, 15.5 us)
Async XLA Ops:
  6.5 190.0 %all-gather.11.cloned.1.call-start = ((), (), s32[]{:S(2)}) async-start(), calls=%async_computation | async-start | bytes 1081344 | tf_op jit(solution)/shard_map/all_gather | solution.py:113
  12.9 9.8 %copy-start.6 = (f32[4,2,4]{2,1,0:T(2,128)S(1)}, f32[4,2,4]{2,1,0:T(2,128)}, u32[]{:S(2)}) copy-start(f32[4,2,4]{2,1,0:T(2,128)} %param.27) | copy-start | bytes 388
  12.9 9.8 %copy-start.7 = (s32[4,128]{1,0:T(4,128)S(1)}, s32[4,128]{1,0:T(4,128)}, u32[]{:S(2)}) copy-start(s32[4,128]{1,0:T(4,128)} %param.26) | copy-start | bytes 6148
  12.9 9.8 %copy-start.8 = (f32[4,128]{1,0:T(4,128)S(1)}, f32[4,128]{1,0:T(4,128)}, u32[]{:S(2)}) copy-start(f32[4,128]{1,0:T(4,128)} %param.23) | copy-start | bytes 6148
  12.9 9.9 %copy-start.5 = (f32[4,3,128]{2,0,1:T(4,128)S(1)}, f32[4,3,128]{2,0,1:T(4,128)}, u32[]{:S(2)}) copy-start(f32[4,3,128]{2,0,1:T(4,128)} %param.24) | copy-start | bytes 18436
  23.6 251.7 %all-gather.13.cloned.1.call-start = ((), (), s32[]{:S(2)}) async-start(), calls=%async_computation.1 | async-start | bytes 1081344 | tf_op jit(solution)/shard_map/all_gather | solution.py:113
  26.8 326.6 %all-gather.15.cloned.1.call-start = ((), (), s32[]{:S(2)}) async-start(), calls=%async_computation.2 | async-start | bytes 1081344 | tf_op jit(solution)/shard_map/all_gather | solution.py:113
  27.6 9.6 %copy-start.4 = (bf16[4,3,128]{2,0,1:T(4,128)(2,1)S(1)}, bf16[4,3,128]{2,0,1:T(4,128)(2,1)}, u32[]{:S(2)}) copy-start(bf16[4,3,128]{2,0,1:T(4,128)(2,1)} %param.22) | copy-start | bytes 9220
  28.3 168.2 %copy-start.1 = (bf16[3,512]{1,0:T(4,128)(2,1)S(1)}, bf16[3,512]{1,0:T(4,128)(2,1)}, u32[]{:S(2)}) copy-start(bf16[3,512]{1,0:T(4,128)(2,1)} %param.20) | copy-start | bytes 9220
  33.9 397.9 %all-gather.17.cloned.1.call-start = ((), (), s32[]{:S(2)}) async-start(), calls=%async_computation.3 | async-start | bytes 1081344 | tf_op jit(solution)/shard_map/all_gather | solution.py:113
  37.2 510.7 %all-gather.19.cloned.1.call-start = ((), (), s32[]{:S(2)}) async-start(), calls=%async_computation.4 | async-start | bytes 2359296 | tf_op jit(solution)/shard_map/all_gather | solution.py:13
  431.8 79.5 %copy-start.9 = (f32[512]{0:T(512)S(1)}, f32[512]{0:T(512)}, u32[]{:S(2)}) copy-start(f32[512]{0:T(512)} %param.21) | copy-start | bytes 6148
  431.8 79.5 %copy-start.3 = (f32[8,512]{1,0:T(8,128)S(1)}, f32[8,512]{1,0:T(8,128)}, u32[]{:S(2)}) copy-start(f32[8,512]{1,0:T(8,128)} %param.30) | copy-start | bytes 49156
  510.5 0.7 copy-start
  551.1 12.5 %copy-start.2 = (s32[8]{0:T(128)S(1)}, s32[8]{0:T(128)}, u32[]{:S(2)}) copy-start(s32[8]{0:T(128)} %param.31) | copy-start | bytes 100
  551.7 22.5 %collective-permute-start.1 = (f32[8,128]{0,1:T(8,128)S(1)}, f32[8,128]{0,1:T(8,128)S(1)}, u32[]{:S(2)}, u32[]{:S(2)}) collective-permute-start(f32[8,128]{0,1:T(8,128)S(1)} %get-tuple-element.580), channel_id=1, source_target_pairs={{8,0},{16,8},{24,16},{32,24},{40,32},{48,40},{56,48},{64,56},{72,6... | collective-permute-start | bytes 12296 | tf_op jit(solution)/shard_map/ppermute | solution.py:25
  559.3 14.9 %collective-permute-start = (f32[8,128]{0,1:T(8,128)S(1)}, f32[8,128]{0,1:T(8,128)S(1)}, u32[]{:S(2)}, u32[]{:S(2)}) collective-permute-start(f32[8,128]{0,1:T(8,128)S(1)} %get-tuple-element.579), channel_id=1, source_target_pairs={{0,8},{8,16},{16,24},{24,32},{32,40},{40,48},{48,56},{56,64},{64,7... | collective-permute-start | bytes 12296 | tf_op jit(solution)/shard_map/ppermute | solution.py:22
Sparse Core Ops, SparseCore 0:
  23.7 76.4 all-gather.10
  102.7 70.0 all-gather.12
  175.4 69.8 all-gather.14
  247.7 69.9 all-gather.16
  511.4 36.4 all-gather.18
